TPU v7x, 32 devices: a whole 2x2x4 slice. The times are simulated.
32 devices in a mesh: dp: 8 (over y, x, core), mp: 4 (over z).
Axes of the slice: x: 2, y: 2, z: 4, core: 2. Of those that a mesh axis runs over, the one named last changes fastest.
Arguments:
- inputs: bfloat16 [8192, 2048], P('dp'), may hold values from -8 to 8
- segment_ids: int32 [8, 1024], P('dp'), may hold values from 0 to 4, as said below
- pad_count: int32 [8], P('dp'), may hold values from 0 to 128, as said below
- layer_norm_gain: float32 [2048], replicated, may hold values from 0.5 to 1.5
- layer_norm_bias: float32 [2048], replicated, may hold values from -1.75 to 1.75
- qkv_weight: bfloat16 [2048, 3, 2048], P(None, None, 'mp'), may hold values from -0.125 to 0.125
- qkv_bias: float32 [3, 2048], P(None, 'mp'), may hold values from -1.75 to 1.75
- out_weight: bfloat16 [2048, 2048], P('mp'), may hold values from -1 to 1
- gateup_weight: bfloat16 [2048, 2, 5632], P(None, None, 'mp'), may hold values from -0.125 to 0.125
- down_weight: bfloat16 [5632, 2048], P('mp'), may hold values from -0.078125 to 0.078125
- y_grad: bfloat16 [8192, 2048], P('dp'), may hold values from -8 to 8
Outputs:
- output: bfloat16 [8192, 2048], P('dp')
- x_grad: bfloat16 [8192, 2048], P('dp')
- ln_gain_grad: float32 [2048], replicated
- ln_bias_grad: float32 [2048], replicated
- qkv_weight_grad: float32 [2048, 3, 2048], P('dp', None, 'mp')
- qkv_bias_grad: float32 [3, 2048], P(None, 'mp')
- out_weight_grad: float32 [2048, 2048], P('mp', 'dp')
- gateup_weight_grad: float32 [2048, 2, 5632], P('dp', None, 'mp')
- down_weight_grad: float32 [5632, 2048], P('mp', 'dp')
Inputs may be any that keep to these rules, and one draw needn't show every extreme that they name: `segment_ids`: within a row the ids never fall and run from 0 to 4 - 1 over the row's documents, each of 1 or more tokens and one of exactly 512; the row's last pad_count slots carry id 4. `pad_count`: some row has 128 padded slots and some row has none.
All inputs are finite; a program needn't handle non-finite values.
Results may differ from a plain program's by a relative error of at most 0.012.
The roundings to bfloat16 on the way count: a program that leaves them out, or rounds other values in their place, can miss the bound.
Values may be sent and summed in bfloat16 or wider, within the bound.
No kernel may reach another device: no remote copies, remote signals or barrier semaphores. Data moves between devices by JAX's collectives and lax.ppermute only.
A program may use at most 256 MiB of HBM per device.

v0:
```python
import jax
import jax.numpy as jnp
from jax import lax
from jax.sharding import PartitionSpec as P

HEAD_DIM = 64
ROT = 16
DOCS = 4
EPS = 1e-05


def tables(seg, padding, count):
    steps = jnp.arange(count, dtype=jnp.int32)
    onehot = (seg[:, None] == jnp.arange(DOCS + 1, dtype=jnp.int32)[None, :]).astype(jnp.int32)
    counts = jnp.sum(onehot, axis=0)
    before = jnp.cumsum(counts) - counts
    start = jnp.sum(onehot * before[None, :], axis=1)
    half = ROT // 2
    freq = jnp.power(10000.0, -2.0 * jnp.arange(half, dtype=jnp.float32) / ROT)
    angle = (steps - start).astype(jnp.float32)[:, None] * freq[None, :]
    return (jnp.cos(angle)[:, None, :], jnp.sin(angle)[:, None, :], steps < count - padding)


def rotate(value, cosine, sine):
    half = ROT // 2
    first = value[..., :half]
    second = value[..., half:ROT]
    return jnp.concatenate(
        [first * cosine - second * sine, second * cosine + first * sine, value[..., ROT:]], axis=-1
    )


def unrotate(value, cosine, sine):
    half = ROT // 2
    first = value[..., :half]
    second = value[..., half:ROT]
    return jnp.concatenate(
        [first * cosine + second * sine, second * cosine - first * sine, value[..., ROT:]], axis=-1
    )


def allowed_mask(start, block_rows, seg, valid):
    count = seg.shape[0]
    rows = start + jnp.arange(block_rows, dtype=jnp.int32)
    cols = jnp.arange(count, dtype=jnp.int32)
    seg_rows = lax.dynamic_slice_in_dim(seg, start, block_rows, 0)
    allowed = (
        (seg_rows[:, None] == seg[None, :]) & (cols[None, :] <= rows[:, None]) & valid[None, :]
    )
    return allowed | (cols[None, :] == rows[:, None])


def scores(start, block_rows, query, key, seg, valid):
    part = lax.dynamic_slice_in_dim(query, start, block_rows, 0)
    score = jnp.einsum(
        "qhd,khd->hqk", part, key, preferred_element_type=jnp.float32
    ) * HEAD_DIM ** (-0.5)
    allowed = allowed_mask(start, block_rows, seg, valid)
    return (part, jnp.where(allowed[None], score, -1e30), allowed)


def shards(
    inputs,
    segment_ids,
    pad_count,
    layer_norm_gain,
    layer_norm_bias,
    qkv_weight,
    qkv_bias,
    out_weight,
    gateup_weight,
    down_weight,
    y_grad,
):
    count, width = inputs.shape
    local = qkv_weight.shape[2]
    hidden_here = gateup_weight.shape[2]
    heads_here = local // HEAD_DIM
    seg = segment_ids[0]
    cosine, sine, valid = tables(seg, pad_count[0], count)
    valid_f = valid.astype(jnp.float32)
    xf = inputs.astype(jnp.float32)
    row_average = jnp.mean(xf, axis=-1, keepdims=True)
    mean_removed = xf - row_average
    var = jnp.mean(mean_removed * mean_removed, axis=-1, keepdims=True)
    inverse_deviation = lax.rsqrt(var + EPS)
    standardized_input = mean_removed * inverse_deviation
    norm_output = (standardized_input * layer_norm_gain + layer_norm_bias).astype(jnp.bfloat16)
    qkv = jnp.dot(
        norm_output, qkv_weight.reshape(width, 3 * local), preferred_element_type=jnp.float32
    )
    qkv = qkv.reshape(count, 3, local) + qkv_bias
    query = rotate(qkv[:, 0].reshape(count, heads_here, HEAD_DIM), cosine, sine).astype(
        jnp.bfloat16
    )
    key = rotate(qkv[:, 1].reshape(count, heads_here, HEAD_DIM), cosine, sine).astype(jnp.bfloat16)
    value = qkv[:, 2].reshape(count, heads_here, HEAD_DIM).astype(jnp.bfloat16)
    block_rows = min(512, count)
    starts = jnp.arange(count // block_rows, dtype=jnp.int32) * block_rows

    def forward_block(start):
        part, score, allowed = scores(start, block_rows, query, key, seg, valid)
        top = jnp.max(score, axis=-1, keepdims=True)
        expo = jnp.exp(score - top)
        total = jnp.sum(expo, axis=-1, keepdims=True)
        prob = (expo / total).astype(jnp.bfloat16)
        return (
            jnp.einsum("hqk,khd->qhd", prob, value, preferred_element_type=jnp.float32),
            (top + jnp.log(total))[..., 0],
        )

    attn_blocks, log_sums = lax.map(forward_block, starts)
    attn = (attn_blocks.reshape(count, local) * valid_f[:, None]).astype(jnp.bfloat16)
    gateup = jnp.dot(
        norm_output,
        gateup_weight.reshape(width, 2 * hidden_here),
        preferred_element_type=jnp.float32,
    )
    gateup = gateup.reshape(count, 2, hidden_here)
    gate = gateup[:, 0]
    upper = gateup[:, 1]
    sigma = jax.nn.sigmoid(gate)
    active = gate * sigma
    hidden = (active * upper).astype(jnp.bfloat16)
    partial_value = jnp.dot(attn, out_weight, preferred_element_type=jnp.float32) + jnp.dot(
        hidden, down_weight, preferred_element_type=jnp.float32
    )
    summed = lax.psum(partial_value, "mp")
    result = (xf + summed).astype(jnp.bfloat16)
    grad_out = jnp.einsum("ti,to->io", attn, y_grad, preferred_element_type=jnp.float32)
    grad_down = jnp.einsum("tf,to->fo", hidden, y_grad, preferred_element_type=jnp.float32)
    d_attn = jnp.einsum("to,io->ti", y_grad, out_weight, preferred_element_type=jnp.float32)
    d_attn = (d_attn.astype(jnp.bfloat16) * valid.astype(jnp.bfloat16)[:, None]).reshape(
        count, heads_here, HEAD_DIM
    )
    d_hidden = jnp.einsum("to,fo->tf", y_grad, down_weight, preferred_element_type=jnp.float32)
    d_gate = (d_hidden * upper * sigma * (1.0 + gate * (1.0 - sigma))).astype(jnp.bfloat16)
    d_upper = (d_hidden * active).astype(jnp.bfloat16)
    d_gateup = jnp.stack([d_gate, d_upper], axis=1)
    grad_gateup = jnp.einsum(
        "td,tjf->djf", norm_output, d_gateup, preferred_element_type=jnp.float32
    )

    def backward_block(carry, item):
        key_acc, value_acc = carry
        start, log_sum = item
        part, score, allowed = scores(start, block_rows, query, key, seg, valid)
        prob = jnp.where(allowed[None], jnp.exp(score - log_sum[..., None]), 0.0)
        prob_low = prob.astype(jnp.bfloat16)
        d_rows = lax.dynamic_slice_in_dim(d_attn, start, block_rows, 0)
        d_prob = jnp.einsum("qhd,khd->hqk", d_rows, value, preferred_element_type=jnp.float32)
        d_score = prob * (d_prob - jnp.sum(prob * d_prob, axis=-1, keepdims=True))
        d_score = d_score.astype(jnp.bfloat16)
        d_query = jnp.einsum(
            "hqk,khd->qhd", d_score, key, preferred_element_type=jnp.float32
        ) * HEAD_DIM ** (-0.5)
        key_acc = key_acc + jnp.einsum(
            "hqk,qhd->khd", d_score, part, preferred_element_type=jnp.float32
        ) * HEAD_DIM ** (-0.5)
        value_acc = value_acc + jnp.einsum(
            "hqk,qhd->khd", prob_low, d_rows, preferred_element_type=jnp.float32
        )
        return ((key_acc, value_acc), d_query)

    empty = jnp.zeros((count, heads_here, HEAD_DIM), jnp.float32)
    (d_key, d_value), d_queries = lax.scan(backward_block, (empty, empty), (starts, log_sums))
    d_query = unrotate(d_queries.reshape(count, heads_here, HEAD_DIM), cosine, sine)
    d_key = unrotate(d_key, cosine, sine)
    d_qkv = (
        jnp.stack([d_query, d_key, d_value], axis=1).reshape(count, 3, local).astype(jnp.bfloat16)
    )
    grad_qkv = jnp.einsum("td,tjc->djc", norm_output, d_qkv, preferred_element_type=jnp.float32)
    grad_bias = jnp.sum(d_qkv.astype(jnp.float32), axis=0)
    weight_sums = (
        lax.psum_scatter(grad_qkv, "dp", scatter_dimension=0, tiled=True),
        lax.psum_scatter(grad_out, "dp", scatter_dimension=1, tiled=True),
        lax.psum_scatter(grad_gateup, "dp", scatter_dimension=0, tiled=True),
        lax.psum_scatter(grad_down, "dp", scatter_dimension=1, tiled=True),
    )
    d_partial = jnp.einsum(
        "tjc,djc->td", d_qkv, qkv_weight, preferred_element_type=jnp.float32
    ) + jnp.einsum("tjf,djf->td", d_gateup, gateup_weight, preferred_element_type=jnp.float32)
    normalized_gradient = lax.psum(d_partial, "mp")
    gain_product = jnp.sum(normalized_gradient * standardized_input, axis=0)
    shift_part = jnp.sum(normalized_gradient, axis=0)
    gain_scaled = normalized_gradient * layer_norm_gain
    inner = (
        gain_scaled
        - jnp.mean(gain_scaled, axis=-1, keepdims=True)
        - standardized_input * jnp.mean(gain_scaled * standardized_input, axis=-1, keepdims=True)
    )
    input_grad = (y_grad.astype(jnp.float32) + inverse_deviation * inner).astype(jnp.bfloat16)
    bias_sum, gain_sum, shift_sum = lax.psum((grad_bias, gain_product, shift_part), "dp")
    return (
        result,
        input_grad,
        gain_sum,
        shift_sum,
        weight_sums[0],
        bias_sum,
        weight_sums[1],
        weight_sums[2],
        weight_sums[3],
    )


def solution(mesh):
    placed = (
        P("dp", None),
        P("dp", None),
        P("dp"),
        P(),
        P(),
        P(None, None, "mp"),
        P(None, "mp"),
        P("mp", None),
        P(None, None, "mp"),
        P("mp", None),
        P("dp", None),
    )
    return jax.shard_map(
        shards,
        mesh=mesh,
        in_specs=placed,
        out_specs=(
            P("dp", None),
            P("dp", None),
            P(),
            P(),
            P("dp", None, "mp"),
            P(None, "mp"),
            P("mp", "dp"),
            P("dp", None, "mp"),
            P("mp", "dp"),
        ),
        check_vma=False,
    )
```

profile of v0, /device:TPU:0, one launch (start us, length us, event | category | flops | bytes accessed | tf_op | source)
XLA Modules:
  0.0 1045.4 jit_solution(3423792791581384292)
XLA Ops:
  8.1 3.0 convert_reduce_fusion
  12.9 8.9 copy.39
  21.8 10.5 %broadcast_add_fusion = f32[1024,3,512]{0,2,1:T(8,128)S(1)} fusion(f32[3,512]{1,0:T(4,128)S(1)} %copy-done.24, bf16[2048,3,512]{0,2,1:T(8,128)(2,1)} %copy.39, bf16[1024,2048]{1,0:T(8,128)(2,1)} %param.15, f32[2048]{0:T(1024)S(1)} %copy-done.25, f32[2048]{0:T(1024)S(1)} %copy-done.21, f32[1024]{0:T(1024)S(1)} %add_rsqrt_fusion, ...), kind=kOutput, calls=%fused_computation.86 | convolution fusion | flops 6456606720 | bytes 16807936 | tf_op jit(solution)/shard_map/dot_general | solution.py:89
  32.4 2.3 fusion.75
  36.2 1.5 slice.130
  37.8 1.5 slice.131
  40.7 1.3 subtract_convert_fusion.2
  43.3 2.0 broadcast.229.clone2
  45.3 79.3 %while.28 = (s32[]{:T(128)}, f32[2,512,8,64]{1,0,3,2:T(2,128)}, f32[2,8,512]{2,1,0:T(8,128)S(1)}, s32[2]{0:T(128)S(1)}, s32[1024]{0:T(1024)S(1)}, /*index=5*/s32...) while((s32[]{:T(128)}, f32[2,512,8,64]{1,0,3,2:T(2,128)}, ...), condition=%wide.region_8.9_spmd.clone, body=%wide.region_5.8_spmd.clone.sunk | while | flops 1127216640 | bytes 64635104 | solution.py:112
  49.9 4.7 fusion.118
  54.6 4.2 fusion.119
  58.9 4.6 fusion.120
  63.5 2.0 copy.73
  65.5 19.6 %dynamic_update_slice.19 = f32[2,512,8,64]{1,0,3,2:T(2,128)} dynamic-update-slice(f32[2,512,8,64]{1,0,3,2:T(2,128)} %get-tuple-element.475, f32[1,512,8,64]{1,0,3,2:T(1,128)} %copy.73, s32[]{:T(128)} %get-tuple-element.474, s32[]{:T(128)} %constant.40.clone.1..sunk, s32[]{:T(128)} %constant.40.clone.1..sunk, s32[]{:T(128)} %constant.40.clone.1..sunk) | dynamic-update-slice | bytes 2097156 | tf_op jit(solution)/shard_map/while/body/jit(dynamic_update_index_in_dim)/dynamic_update_slice | solution.py:112
  89.3 4.7 fusion.118
  94.0 4.2 fusion.119
  98.3 4.6 fusion.120
  102.8 2.0 copy.73
  104.9 19.6 %dynamic_update_slice.19 = f32[2,512,8,64]{1,0,3,2:T(2,128)} dynamic-update-slice(f32[2,512,8,64]{1,0,3,2:T(2,128)} %get-tuple-element.475, f32[1,512,8,64]{1,0,3,2:T(1,128)} %copy.73, s32[]{:T(128)} %get-tuple-element.474, s32[]{:T(128)} %constant.40.clone.1..sunk, s32[]{:T(128)} %constant.40.clone.1..sunk, s32[]{:T(128)} %constant.40.clone.1..sunk) | dynamic-update-slice | bytes 2097156 | tf_op jit(solution)/shard_map/while/body/jit(dynamic_update_index_in_dim)/dynamic_update_slice | solution.py:112
  124.5 5.5 fusion.62
  130.1 2.0 broadcast.229.clone
  132.1 159.0 %while.29 = (s32[]{:T(128)}, f32[1024,8,64]{0,2,1:T(8,128)}, f32[1024,8,64]{0,2,1:T(8,128)}, f32[2,512,8,64]{1,0,3,2:T(2,128)}, s32[2]{0:T(128)S(1)}, /*index=5*...) while((s32[]{:T(128)}, f32[1024,8,64]{0,2,1:T(8,128)}, ...), condition=%wide.region_12.13_spmd.clone, body=%wide.region_10.12_spmd.clone.sunk | while | flops 2732324352 | bytes 187793712 | solution.py:166
  136.4 9.7 fusion.130
  146.1 13.8 %multiply_reduce_fusion.3 = (f32[8,512]{1,0:T(8,128)S(1)}, f32[8,512,1024]{2,1,0:T(8,128)}) fusion(f32[8,512,1024]{2,1,0:T(8,128)} %fusion.130, f32[8,512]{1,0:T(8,128)S(1)} %dynamic-slice_bitcast_fusion.2, bf16[1024,8,64]{0,2,1:T(8,128)(2,1)S(1)} %get-tuple-element.540, bf16[1024,8,64]{0,2,1:T(8,128)(2,1)S(1)} %copy-done.4, s32[]{:T(128)S(6)} %select_n.47, ...), kind=kOutput, calls=%fused_computation.23.clone.1 | convolution fusion | flops 562032640 | bytes 35684356 | tf_op jit(solution)/shard_map/while/body/eval_jaxpr/qhd,khd->hqk/dot_general | solution.py:55
  159.9 11.3 %multiply_convert_fusion.8 = bf16[8,512,1024]{2,1,0:T(8,128)(2,1)S(1)} fusion(f32[8,512,1024]{2,1,0:T(8,128)} %get-tuple-element.459, f32[8,512,1024]{2,1,0:T(8,128)} %fusion.130, f32[8,512]{1,0:T(8,128)S(1)} %get-tuple-element.460), kind=kLoop, calls=%fused_computation.22.clone.1 | loop fusion | flops 12582912 | bytes 41959424 | tf_op jit(solution)/shard_map/while/body/eval_jaxpr/convert_element_type | solution.py:153
  171.2 2.7 fusion.132
  173.9 2.1 copy.74
  176.0 19.6 %dynamic_update_slice.20 = f32[2,512,8,64]{1,0,3,2:T(2,128)} dynamic-update-slice(f32[2,512,8,64]{1,0,3,2:T(2,128)} %get-tuple-element.519, f32[1,512,8,64]{1,0,3,2:T(1,128)} %copy.74, s32[]{:T(128)} %get-tuple-element.516, s32[]{:T(128)} %constant.40.clone.1..sunk.1, s32[]{:T(128)} %constant.40.clone.1..sunk.1, s32[]{:T(128)} %constant.40.clone.1..sunk.1) | dynamic-update-slice | bytes 2097156 | tf_op jit(solution)/shard_map/while/body/jit(dynamic_update_index_in_dim)/dynamic_update_slice | solution.py:112
  195.6 6.6 bitcast_add_fusion.5
  202.3 8.7 bitcast_add_fusion.6
  215.2 9.7 fusion.130
  224.8 13.7 %multiply_reduce_fusion.3 = (f32[8,512]{1,0:T(8,128)S(1)}, f32[8,512,1024]{2,1,0:T(8,128)}) fusion(f32[8,512,1024]{2,1,0:T(8,128)} %fusion.130, f32[8,512]{1,0:T(8,128)S(1)} %dynamic-slice_bitcast_fusion.2, bf16[1024,8,64]{0,2,1:T(8,128)(2,1)S(1)} %get-tuple-element.540, bf16[1024,8,64]{0,2,1:T(8,128)(2,1)S(1)} %copy-done.4, s32[]{:T(128)S(6)} %select_n.47, ...), kind=kOutput, calls=%fused_computation.23.clone.1 | convolution fusion | flops 562032640 | bytes 35684356 | tf_op jit(solution)/shard_map/while/body/eval_jaxpr/qhd,khd->hqk/dot_general | solution.py:55
  238.6 11.3 %multiply_convert_fusion.8 = bf16[8,512,1024]{2,1,0:T(8,128)(2,1)S(1)} fusion(f32[8,512,1024]{2,1,0:T(8,128)} %get-tuple-element.459, f32[8,512,1024]{2,1,0:T(8,128)} %fusion.130, f32[8,512]{1,0:T(8,128)S(1)} %get-tuple-element.460), kind=kLoop, calls=%fused_computation.22.clone.1 | loop fusion | flops 12582912 | bytes 41959424 | tf_op jit(solution)/shard_map/while/body/eval_jaxpr/convert_element_type | solution.py:153
  249.9 2.7 fusion.132
  252.6 2.1 copy.74
  254.7 19.6 %dynamic_update_slice.20 = f32[2,512,8,64]{1,0,3,2:T(2,128)} dynamic-update-slice(f32[2,512,8,64]{1,0,3,2:T(2,128)} %get-tuple-element.519, f32[1,512,8,64]{1,0,3,2:T(1,128)} %copy.74, s32[]{:T(128)} %get-tuple-element.516, s32[]{:T(128)} %constant.40.clone.1..sunk.1, s32[]{:T(128)} %constant.40.clone.1..sunk.1, s32[]{:T(128)} %constant.40.clone.1..sunk.1) | dynamic-update-slice | bytes 2097156 | tf_op jit(solution)/shard_map/while/body/jit(dynamic_update_index_in_dim)/dynamic_update_slice | solution.py:112
  274.3 7.2 bitcast_add_fusion.5
  281.5 9.3 bitcast_add_fusion.6
  291.1 4.1 reshape.378
  295.2 1.5 slice.129
  298.0 2.4 slice.128
  300.5 1.3 copy.43
  303.1 1.3 copy.44
  304.4 1.7 convert.64
  306.2 1.3 copy.45
  307.5 11.2 %copy.66 = bf16[256,8,2,1408]{3,1,2,0:T(8,128)(2,1)} copy(bf16[256,8,2,1408]{3,2,1,0:T(2,128)(2,1)} %bitcast.147) | data formatting | bytes 23068672
  318.8 15.2 %copy.41 = bf16[2816,2048]{1,0:T(8,128)(2,1)} copy(bf16[2816,2048]{0,1:T(8,128)(2,1)} %bitcast.143) | data formatting | bytes 23068672 | tf_op jit(solution)/shard_map/dot_general | solution.py:114
  334.0 19.1 %fusion.72 = f32[1024,2,1408]{2,0,1:T(8,128)} fusion(bf16[2,1408,2048]{2,1,0:T(8,128)(2,1)} %bitcast.148, bf16[1024,2048]{1,0:T(8,128)(2,1)} %param.15, f32[2048]{0:T(1024)S(1)} %copy-done.26, f32[2048]{0:T(1024)S(1)} %copy-done.22, f32[1024]{0:T(1024)S(1)} %copy-done.20, f32[1024]{0:T(1024)S(1)} %copy-done.18), kind=kOutput, calls=%fused_computation.130 | convolution fusion | flops 11823742976 | bytes 27287552 | tf_op jit(solution)/shard_map/dot_general | solution.py:114
  353.6 17.5 %fusion.59 = (bf16[1024,1,1408]{2,0,1:T(8,128)(2,1)}, bf16[1024,1,1408]{2,0,1:T(8,128)(2,1)}, bf16[1024,1408]{1,0:T(8,128)(2,1)}) fusion(f32[1024,2,1408]{2,0,1:T(8,128)} %fusion.72, bf16[1024,2048]{1,0:T(8,128)(2,1)} %param.25, bf16[1408,2048]{1,0:T(8,128)(2,1)} %param.24), kind=kOutput, calls=%fused_computation.88 | convolution fusion | flops 5927206912 | bytes 30146560 | tf_op jit(solution)/shard_map/to,fo->tf/dot_general | solution.py:136
  371.1 12.3 %fusion.76 = f32[1024,2048]{1,0:T(8,128)} fusion(bf16[1024,1408]{1,0:T(8,128)(2,1)} %get-tuple-element.292, bf16[1408,2048]{1,0:T(8,128)(2,1)} %param.24), kind=kOutput, calls=%fused_computation.132 | convolution fusion | flops 5905580032 | bytes 17039360 | tf_op jit(solution)/shard_map/dot_general | solution.py:125
  383.5 8.9 fusion.69
  392.4 20.2 %bitcast_add_fusion.2 = f32[1024,2048]{1,0:T(8,128)} fusion(f32[1024,2048,1]{1,0,2:T(8,128)} %fusion.69, bf16[2048,2,1408]{2,1,0:T(2,128)(2,1)} %param.23, bf16[1024,1,1408]{2,0,1:T(8,128)(2,1)} %get-tuple-element.291, bf16[1024,1,1408]{2,0,1:T(8,128)(2,1)} %get-tuple-element.290), kind=kOutput, calls=%fused_computation.69 | convolution fusion | flops 11816140800 | bytes 34078720 | tf_op jit(solution)/shard_map/tjf,djf->td/dot_general | solution.py:182
  412.7 9.1 convolution_add_fusion
  421.8 20.7 %fusion.57 = f32[2048,2,1408]{2,0,1:T(8,128)} fusion(bf16[1024,1,1408]{2,0,1:T(8,128)(2,1)} %get-tuple-element.291, bf16[1024,1,1408]{2,0,1:T(8,128)(2,1)} %get-tuple-element.290, bf16[1024,2048]{1,0:T(8,128)(2,1)} %param.15, f32[2048]{0:T(1024)S(1)} %copy-done.26, f32[2048]{0:T(1024)S(1)} %copy-done.22, f32[1024]{0:T(1024)S(1)} %copy-done.20, ...), kind=kOutput, calls=%fused_computation.84 | convolution fusion | flops 11835277312 | bytes 33054720 | tf_op jit(solution)/shard_map/td,tjf->djf/dot_general | solution.py:140
  442.6 7.1 fusion.63
  449.8 13.8 %fusion.77 = f32[1408,2048]{1,0:T(8,128)} fusion(bf16[1024,1408]{1,0:T(8,128)(2,1)} %get-tuple-element.292, bf16[1024,2048]{1,0:T(8,128)(2,1)} %param.25), kind=kOutput, calls=%fused_computation.133 | convolution fusion | flops 5905580032 | bytes 18612224 | tf_op jit(solution)/shard_map/tf,to->fo/dot_general | solution.py:131
  463.6 1.4 copy-done.9
  465.0 15.0 %fusion.68 = f32[2048,3,512]{2,0,1:T(8,128)} fusion(bf16[1024,1,512]{2,0,1:T(8,128)(2,1)} %copy.45, bf16[1024,1,512]{2,0,1:T(8,128)(2,1)} %copy.44, bf16[1024,1,512]{2,0,1:T(8,128)(2,1)S(1)} %copy-done.9, bf16[1024,2048]{1,0:T(8,128)(2,1)} %param.15, f32[2048]{0:T(1024)S(1)} %copy-done.26, f32[2048]{0:T(1024)S(1)} %copy-done.22, f32[1024]{0:T(1024)S(1)} %copy-done.20, ...), kind=kOutput, calls=%fused_computation.128 | convolution fusion | flops 6464471040 | bytes 19947520 | tf_op jit(solution)/shard_map/td,tjc->djc/dot_general | solution.py:172
  480.1 2.0 convert_reduce_fusion.1
  482.1 504.8 %all-reduce.4.cloned.1.call-done = (f32[1024,2048]{1,0:T(8,128)}, f32[1024,2048]{1,0:T(8,128)}) async-done(((f32[1024,2048]{1,0:T(8,128)}, f32[1024,2048]{1,0:T(8,128)}), (f32[1024,2048]{1,0:T(8,128)}, f32[1024,2048]{1,0:T(8,128)})) %all-reduce.4.cloned.1.call-update) | async-done | bytes 16777232 | tf_op jit(solution)/shard_map/psum | solution.py:128
  986.9 6.5 fusion.48
  993.4 24.8 %all-reduce = (f32[2048]{0:T(1024)}, f32[2048]{0:T(1024)}, f32[3,512]{1,0:T(4,128)}) all-reduce(f32[2048]{0:T(1024)S(1)} %get-tuple-element.231, f32[2048]{0:T(1024)S(1)} %get-tuple-element.234, f32[3,512]{1,0:T(4,128)S(1)} %convert_reduce_fusion.1), channel_id=1, replica_groups=mesh['dp'=8,'mp'=4] {'dp'}, use_global_device_ids=true, to_apply=%region_17.18 | all-reduce | flops 5632 | bytes 45056 | tf_op jit(solution)/shard_map/psum | solution.py:193
  1018.2 13.6 %fusion.47 = (bf16[1024,2048]{1,0:T(8,128)(2,1)}, bf16[1024,2048]{1,0:T(8,128)(2,1)}) fusion(bf16[1024,2048]{1,0:T(8,128)(2,1)} %param.15, bf16[1024,2048]{1,0:T(8,128)(2,1)} %param.25, f32[1024,2048]{1,0:T(8,128)} %get-tuple-element.285, f32[1024]{0:T(1024)S(1)} %broadcast_multiply_fusion, f32[1024]{0:T(1024)S(1)} %broadcast_multiply_fusion.1, ...), kind=kLoop, calls=%fused_computation.65 | loop fusion | flops 27262976 | bytes 33579008 | tf_op jit(solution)/shard_map/convert_element_type | solution.py:192
  1031.9 5.6 copy.49
  (128 shorter events, 17.6 us)
Async XLA Ops:
  8.0 116.5 %copy-start = (bf16[512,2048]{1,0:T(8,128)(2,1)S(1)}, bf16[512,2048]{1,0:T(8,128)(2,1)}, u32[]{:S(2)}) copy-start(bf16[512,2048]{1,0:T(8,128)(2,1)} %param.22) | copy-start | bytes 6291460
  8.0 978.9 %all-reduce.4.cloned.1.call-start = ((), (), s32[]{:S(2)}) async-start(), calls=%async_computation.8 | async-start | bytes 33554432 | tf_op jit(solution)/shard_map/psum | solution.py:128
  8.1 3.6 copy-start.3
  11.7 10.1 copy-start.17
  12.9 8.9 copy-start.19
  12.9 8.9 copy-start.21
  12.9 8.9 copy-start.24
  12.9 8.9 copy-start.25
  32.4 3.5 copy-start.12
  40.7 1.4 copy-start.13
  40.7 1.4 copy-start.15
  45.3 79.3 %copy-start.23 = (bf16[1024]{0:T(1024)(128)(2,1)S(1)}, bf16[1024]{0:T(1024)(128)(2,1)}, u32[]{:S(2)}) copy-start(bf16[1024]{0:T(1024)(128)(2,1)} %fusion.65) | copy-start | bytes 6148
  54.6 4.3 copy-start.2
  94.0 4.3 copy-start.2
  136.4 9.7 copy-start.4
  171.2 4.8 copy-start.1
  195.6 6.6 copy-start.5
  215.1 9.7 copy-start.4
  249.9 4.8 copy-start.1
  274.3 7.2 copy-start.5
  291.1 5.6 copy-start.14
  291.1 5.6 copy-start.16
  318.8 15.2 %copy-start.18 = (f32[1024]{0:T(1024)S(1)}, f32[1024]{0:T(1024)}, u32[]{:S(2)}) copy-start(f32[1024]{0:T(1024)} %copy-done.17) | copy-start | bytes 12292
  318.8 15.2 %copy-start.20 = (f32[1024]{0:T(1024)S(1)}, f32[1024]{0:T(1024)}, u32[]{:S(2)}) copy-start(f32[1024]{0:T(1024)} %copy-done.19) | copy-start | bytes 12292
  318.8 15.2 %copy-start.22 = (f32[2048]{0:T(1024)S(1)}, f32[2048]{0:T(1024)}, u32[]{:S(2)}) copy-start(f32[2048]{0:T(1024)} %param.18) | copy-start | bytes 24580
  318.8 15.2 %copy-start.26 = (f32[2048]{0:T(1024)S(1)}, f32[2048]{0:T(1024)}, u32[]{:S(2)}) copy-start(f32[2048]{0:T(1024)} %param.19) | copy-start | bytes 24580
  334.0 19.1 %copy-start.7 = (f32[2,512,8,64]{1,0,3,2:T(2,128)S(1)}, f32[2,512,8,64]{1,0,3,2:T(2,128)}, u32[]{:S(2)}) copy-start(f32[2,512,8,64]{1,0,3,2:T(2,128)} %get-tuple-element.131) | copy-start | bytes 6291460
  353.1 30.4 %slice-start = ((s8[6291456]{0:T(1024)(128)(4,1)}), s8[4194304]{0:T(1024)(128)(4,1)S(1)}, s32[]{:S(2)}) async-start(s8[6291456]{0:T(1024)(128)(4,1)} %bitcast.150), calls=%async_computation.9 | async-start | bytes 8388608
  353.5 59.2 %copy-start.6 = (f32[64,8,2,512]{3,1,2,0:T(8,128)}, f32[64,8,2,512]{3,1,2,0:T(8,128)S(1)}, u32[]{:S(2)}) copy-start(f32[64,8,2,512]{3,1,2,0:T(8,128)S(1)} %copy.65) | copy-start | bytes 6291460
  353.5 29.9 %slice-start.1 = ((s8[6291456]{0:T(1024)(128)(4,1)}), s8[2097152]{0:T(1024)(128)(4,1)S(1)}, s32[]{:S(2)}) async-start(s8[6291456]{0:T(1024)(128)(4,1)} %bitcast.150), calls=%async_computation.10 | async-start | bytes 4194304
  371.1 12.4 %copy-start.8 = (bf16[1024,1,512]{2,0,1:T(8,128)(2,1)S(1)}, bf16[1024,1,512]{2,0,1:T(8,128)(2,1)}, u32[]{:S(2)}) copy-start(bf16[1024,1,512]{2,0,1:T(8,128)(2,1)} %copy.43) | copy-start | bytes 3145732
  371.1 12.4 %copy-start.10 = (bf16[1024,1,512]{2,0,1:T(8,128)(2,1)S(1)}, bf16[1024,1,512]{2,0,1:T(8,128)(2,1)}, u32[]{:S(2)}) copy-start(bf16[1024,1,512]{2,0,1:T(8,128)(2,1)} %copy.44) | copy-start | bytes 3145732
  371.1 12.4 %copy-start.11 = (bf16[1024,1,512]{2,0,1:T(8,128)(2,1)S(1)}, bf16[1024,1,512]{2,0,1:T(8,128)(2,1)}, u32[]{:S(2)}) copy-start(bf16[1024,1,512]{2,0,1:T(8,128)(2,1)} %copy.45) | copy-start | bytes 3145732
  421.8 610.1 %reduce-scatter.9.cloned.1.call-start = ((), (), s32[]{:S(2)}) async-start(), calls=%async_computation.6 | async-start | bytes 25952256 | tf_op jit(solution)/shard_map/reduce_scatter | solution.py:177
  442.5 595.0 %reduce-scatter.7.cloned.1.call-start = ((), (), s32[]{:S(2)}) async-start(), calls=%async_computation.5 | async-start | bytes 4718592 | tf_op jit(solution)/shard_map/reduce_scatter | solution.py:176
  449.7 587.8 %reduce-scatter.11.cloned.1.call-start = ((), (), s32[]{:S(2)}) async-start(), calls=%async_computation.7 | async-start | bytes 12976128 | tf_op jit(solution)/shard_map/reduce_scatter | solution.py:178
  463.5 1.5 copy-start.9
  463.6 573.9 %reduce-scatter.5.cloned.1.call-start = ((), (), s32[]{:S(2)}) async-start(), calls=%async_computation.4 | async-start | bytes 14155776 | tf_op jit(solution)/shard_map/reduce_scatter | solution.py:175
Sparse Core Ops, SparseCore 0:
  421.9 564.9 all-reduce.3
Sparse Core Ops, SparseCore 1:
  442.6 148.9 reduce-scatter.8
  595.3 50.9 reduce-scatter.6
  650.2 86.7 reduce-scatter.10
  741.0 91.8 reduce-scatter.4
where the time goes:
time: 1060 us; the launch traced here: 1050 us
  waiting for transfers between devices  505 us (48%)
  matrix products  262 us (25%)
  local copies, waits for them, and re-layouts  156 us (15%)
  other arithmetic  71.6 us (7%)
  blocking collectives  24.8 us (2%)
  between operations  17 us (2%)
    psum x1, waiting for transfers between devices, shards(): summed = lax.psum(partial_value, 'mp')  505 us
    dynamic_update_slice x8, local copies, waits for them, and re-layouts, shards(): attn_blocks, log_sums = lax.map(forward_block, starts)  86.9 us
    dot_general x4, matrix products, scores(): jnp.einsum('qhd,khd->hqk', part, key, preferred_element_type=jnp.float32)  36.8 us
    unnamed x54, local copies, waits for them, and re-layouts  28.3 us
    psum x1, blocking collectives, shards(): lax.psum((grad_bias, gain_product, shift_part), 'dp')  24.8 us
    convert_element_type x2, other arithmetic, backward_block(): d_score = d_score.astype(jnp.bfloat16)  22.7 us
  transfers between devices with their start and end apart: 5, of which 1 were waited for; matrix products, arithmetic and copies ran while one was open for 8% of the time, Pallas kernels for 0%

commit v1 on v0

--- a/solution.py
+++ b/solution.py
@@ -125,7 +125,7 @@
     partial_value = jnp.dot(attn, out_weight, preferred_element_type=jnp.float32) + jnp.dot(
         hidden, down_weight, preferred_element_type=jnp.float32
     )
-    summed = lax.psum(partial_value, "mp")
+    summed = jnp.sum(lax.all_gather(partial_value, "mp"), axis=0)
     result = (xf + summed).astype(jnp.bfloat16)
     grad_out = jnp.einsum("ti,to->io", attn, y_grad, preferred_element_type=jnp.float32)
     grad_down = jnp.einsum("tf,to->fo", hidden, y_grad, preferred_element_type=jnp.float32)

time: 1060 us -> 1300 us (1.23)
  waiting for transfers between devices: 505 us -> 735 us
  other arithmetic: 71.6 us -> 91.7 us
    all_gather x0 -> x1, waiting for transfers between devices: none -> 521 us  [shards(): summed = jnp.sum(lax.all_gather(partial_value, 'mp'), axis=0)]
    psum x1, waiting for transfers between devices: 505 us -> 213 us  [shards(): normalized_gradient = lax.psum(d_partial, 'mp')]
    reduce_sum x0 -> x1, other arithmetic: none -> 15.9 us  [shards(): summed = jnp.sum(lax.all_gather(partial_value, 'mp'), axis=0)]
    unnamed x54 -> x46, local copies, waits for them, and re-layouts: 28.3 us -> 29.6 us
  transfers between devices with their start and end apart: 5 -> 6, of which waited for: 1 -> 2; matrix products, arithmetic and copies ran while one was open for 8% -> 10% of each run, Pallas kernels for 0% -> 0%
where the time goes in v1:
time: 1300 us; the launch traced here: 1290 us
  waiting for transfers between devices  735 us (57%)
  matrix products  250 us (19%)
  local copies, waits for them, and re-layouts  161 us (12%)
  other arithmetic  91.7 us (7%)
  blocking collectives  26.3 us (2%)
  between operations  16.9 us (1%)
    all_gather x1, waiting for transfers between devices, shards(): summed = jnp.sum(lax.all_gather(partial_value, 'mp'), axis=0)  521 us
    psum x1, waiting for transfers between devices, shards(): normalized_gradient = lax.psum(d_partial, 'mp')  213 us
    dynamic_update_slice x8, local copies, waits for them, and re-layouts, shards(): attn_blocks, log_sums = lax.map(forward_block, starts)  86.6 us
    dot_general x4, matrix products, scores(): jnp.einsum('qhd,khd->hqk', part, key, preferred_element_type=jnp.float32)  36.8 us
    unnamed x46, local copies, waits for them, and re-layouts  29.6 us
    psum x1, blocking collectives, shards(): lax.psum((grad_bias, gain_product, shift_part), 'dp')  26.3 us
  transfers between devices with their start and end apart: 6, of which 2 were waited for; matrix products, arithmetic and copies ran while one was open for 10% of the time, Pallas kernels for 0%

profile of v1, /device:TPU:0, one launch (start us, length us, event | category | flops | bytes accessed | tf_op | source)
XLA Modules:
  0.0 1290.6 jit_solution(4998599029802011729)
XLA Ops:
  8.1 3.0 convert_reduce_fusion
  13.0 8.8 copy.39
  21.9 10.5 broadcast_add_fusion
  33.5 2.3 fusion.75
  37.5 1.5 slice.131
  39.0 1.5 slice.130
  43.3 2.0 broadcast.229.clone2
  45.3 78.8 %while.28 = (s32[]{:T(128)}, f32[2,512,8,64]{1,0,3,2:T(2,128)}, f32[2,8,512]{2,1,0:T(8,128)S(1)}, s32[2]{0:T(128)S(1)}, s32[1024]{0:T(1024)S(1)}, /*index=5*/s32...) while((s32[]{:T(128)}, f32[2,512,8,64]{1,0,3,2:T(2,128)}, ...), condition=%wide.region_8.9_spmd.clone, body=%wide.region_5.8_spmd.clone.sunk | while | flops 1127216640 | bytes 64635112 | solution.py:112
  49.6 4.7 fusion.118
  54.3 4.2 fusion.119
  58.6 4.6 fusion.120
  63.2 2.0 copy.74
  65.2 19.6 %dynamic_update_slice.19 = f32[2,512,8,64]{1,0,3,2:T(2,128)} dynamic-update-slice(f32[2,512,8,64]{1,0,3,2:T(2,128)} %get-tuple-element.473, f32[1,512,8,64]{1,0,3,2:T(1,128)} %copy.74, s32[]{:T(128)S(6)} %copy.82, s32[]{:T(128)} %constant.40.clone.1..sunk, s32[]{:T(128)} %constant.40.clone.1..sunk, s32[]{:T(128)} %constant.40.clone.1..sunk) | dynamic-update-slice | bytes 2097156 | tf_op jit(solution)/shard_map/while/body/jit(dynamic_update_index_in_dim)/dynamic_update_slice | solution.py:112
  88.9 4.7 fusion.118
  93.6 4.2 fusion.119
  97.9 4.6 fusion.120
  102.5 2.0 copy.74
  104.5 19.6 %dynamic_update_slice.19 = f32[2,512,8,64]{1,0,3,2:T(2,128)} dynamic-update-slice(f32[2,512,8,64]{1,0,3,2:T(2,128)} %get-tuple-element.473, f32[1,512,8,64]{1,0,3,2:T(1,128)} %copy.74, s32[]{:T(128)S(6)} %copy.82, s32[]{:T(128)} %constant.40.clone.1..sunk, s32[]{:T(128)} %constant.40.clone.1..sunk, s32[]{:T(128)} %constant.40.clone.1..sunk) | dynamic-update-slice | bytes 2097156 | tf_op jit(solution)/shard_map/while/body/jit(dynamic_update_index_in_dim)/dynamic_update_slice | solution.py:112
  124.1 5.5 fusion.62
  129.6 2.0 broadcast.229.clone
  131.6 151.9 %while.29 = (s32[]{:T(128)}, f32[1024,8,64]{0,2,1:T(8,128)}, f32[1024,8,64]{0,2,1:T(8,128)}, f32[2,512,8,64]{1,0,3,2:T(2,128)}, s32[2]{0:T(128)S(1)}, /*index=5*...) while((s32[]{:T(128)}, f32[1024,8,64]{0,2,1:T(8,128)}, ...), condition=%wide.region_12.13_spmd.clone, body=%wide.region_10.12_spmd.clone.sunk | while | flops 2732324352 | bytes 171016560 | solution.py:166
  136.0 9.7 fusion.130
  145.7 13.7 %multiply_reduce_fusion.3 = (f32[8,512]{1,0:T(8,128)S(1)}, f32[8,512,1024]{2,1,0:T(8,128)}) fusion(f32[8,512,1024]{2,1,0:T(8,128)} %fusion.130, f32[8,512]{1,0:T(8,128)S(1)} %dynamic-slice_bitcast_fusion.2, bf16[1024,8,64]{0,2,1:T(8,128)(2,1)S(1)} %get-tuple-element.538, bf16[1024,8,64]{0,2,1:T(8,128)(2,1)S(1)} %copy-done.5, s32[]{:T(128)S(6)} %select_n.47, ...), kind=kOutput, calls=%fused_computation.23.clone.1 | convolution fusion | flops 562032640 | bytes 35684356 | tf_op jit(solution)/shard_map/while/body/eval_jaxpr/qhd,khd->hqk/dot_general | solution.py:55
  159.4 11.4 multiply_convert_fusion.8
  170.8 8.8 bitcast_add_fusion.6
  179.6 2.7 fusion.132
  182.3 1.9 bitcast_add_fusion.5
  185.5 2.1 copy.75
  187.5 19.6 %dynamic_update_slice.20 = f32[2,512,8,64]{1,0,3,2:T(2,128)} dynamic-update-slice(f32[2,512,8,64]{1,0,3,2:T(2,128)} %get-tuple-element.517, f32[1,512,8,64]{1,0,3,2:T(1,128)} %copy.75, s32[]{:T(128)S(6)} %copy.92, s32[]{:T(128)} %constant.40.clone.1..sunk.1, s32[]{:T(128)} %constant.40.clone.1..sunk.1, s32[]{:T(128)} %constant.40.clone.1..sunk.1) | dynamic-update-slice | bytes 2097156 | tf_op jit(solution)/shard_map/while/body/jit(dynamic_update_index_in_dim)/dynamic_update_slice | solution.py:112
  211.4 9.7 fusion.130
  221.0 13.7 %multiply_reduce_fusion.3 = (f32[8,512]{1,0:T(8,128)S(1)}, f32[8,512,1024]{2,1,0:T(8,128)}) fusion(f32[8,512,1024]{2,1,0:T(8,128)} %fusion.130, f32[8,512]{1,0:T(8,128)S(1)} %dynamic-slice_bitcast_fusion.2, bf16[1024,8,64]{0,2,1:T(8,128)(2,1)S(1)} %get-tuple-element.538, bf16[1024,8,64]{0,2,1:T(8,128)(2,1)S(1)} %copy-done.5, s32[]{:T(128)S(6)} %select_n.47, ...), kind=kOutput, calls=%fused_computation.23.clone.1 | convolution fusion | flops 562032640 | bytes 35684356 | tf_op jit(solution)/shard_map/while/body/eval_jaxpr/qhd,khd->hqk/dot_general | solution.py:55
  234.8 11.4 multiply_convert_fusion.8
  246.2 9.3 bitcast_add_fusion.6
  255.5 2.7 fusion.132
  258.2 1.9 bitcast_add_fusion.5
  261.4 2.1 copy.75
  263.5 19.6 %dynamic_update_slice.20 = f32[2,512,8,64]{1,0,3,2:T(2,128)} dynamic-update-slice(f32[2,512,8,64]{1,0,3,2:T(2,128)} %get-tuple-element.517, f32[1,512,8,64]{1,0,3,2:T(1,128)} %copy.75, s32[]{:T(128)S(6)} %copy.92, s32[]{:T(128)} %constant.40.clone.1..sunk.1, s32[]{:T(128)} %constant.40.clone.1..sunk.1, s32[]{:T(128)} %constant.40.clone.1..sunk.1) | dynamic-update-slice | bytes 2097156 | tf_op jit(solution)/shard_map/while/body/jit(dynamic_update_index_in_dim)/dynamic_update_slice | solution.py:112
  283.5 4.1 reshape.378
  287.6 2.4 slice.128
  295.4 2.2 pad_maximum_fusion.7
  297.6 2.3 copy.44
  299.9 2.7 convert.64
  302.7 2.3 copy.45
  305.0 11.2 copy.67
  316.2 15.2 %copy.41 = bf16[2816,2048]{1,0:T(8,128)(2,1)} copy(bf16[2816,2048]{0,1:T(8,128)(2,1)} %bitcast.144) | data formatting | bytes 23068672 | tf_op jit(solution)/shard_map/dot_general | solution.py:114
  331.4 19.1 %fusion.72 = f32[1024,2,1408]{2,0,1:T(8,128)} fusion(bf16[2,1408,2048]{2,1,0:T(8,128)(2,1)} %bitcast.150, bf16[1024,2048]{1,0:T(8,128)(2,1)} %param.15, f32[2048]{0:T(1024)S(1)} %copy-done.23, f32[2048]{0:T(1024)S(1)} %copy-done.19, f32[1024]{0:T(1024)S(1)} %copy-done.17, f32[1024]{0:T(1024)S(1)} %copy-done.15), kind=kOutput, calls=%fused_computation.130 | convolution fusion | flops 11823742976 | bytes 27287552 | tf_op jit(solution)/shard_map/dot_general | solution.py:114
  350.6 16.7 %fusion.59 = (bf16[1024,1,1408]{2,0,1:T(8,128)(2,1)}, bf16[1024,1,1408]{2,0,1:T(8,128)(2,1)}, bf16[1024,1408]{1,0:T(8,128)(2,1)}) fusion(f32[1024,2,1408]{2,0,1:T(8,128)} %fusion.72, bf16[1024,2048]{1,0:T(8,128)(2,1)} %param.25, bf16[1408,2048]{1,0:T(8,128)(2,1)} %param.24), kind=kOutput, calls=%fused_computation.88 | convolution fusion | flops 5927206912 | bytes 30146560 | tf_op jit(solution)/shard_map/to,fo->tf/dot_general | solution.py:136
  367.3 10.1 fusion.69
  377.4 20.1 %bitcast_add_fusion.2 = f32[1024,2048]{1,0:T(8,128)} fusion(f32[1024,2048,1]{1,0,2:T(8,128)} %fusion.69, bf16[2048,2,1408]{2,1,0:T(2,128)(2,1)} %param.23, bf16[1024,1,1408]{2,0,1:T(8,128)(2,1)} %get-tuple-element.289, bf16[1024,1,1408]{2,0,1:T(8,128)(2,1)} %get-tuple-element.288), kind=kOutput, calls=%fused_computation.69 | convolution fusion | flops 11816140800 | bytes 34078720 | tf_op jit(solution)/shard_map/tjf,djf->td/dot_general | solution.py:182
  397.6 20.7 %fusion.57 = f32[2048,2,1408]{2,0,1:T(8,128)} fusion(bf16[1024,1,1408]{2,0,1:T(8,128)(2,1)} %get-tuple-element.289, bf16[1024,1,1408]{2,0,1:T(8,128)(2,1)} %get-tuple-element.288, bf16[1024,2048]{1,0:T(8,128)(2,1)} %param.15, f32[2048]{0:T(1024)S(1)} %copy-done.23, f32[2048]{0:T(1024)S(1)} %copy-done.19, f32[1024]{0:T(1024)S(1)} %copy-done.17, ...), kind=kOutput, calls=%fused_computation.84 | convolution fusion | flops 11835277312 | bytes 33054720 | tf_op jit(solution)/shard_map/td,tjf->djf/dot_general | solution.py:140
  418.4 2.1 copy.66
  420.5 10.3 fusion.76
  430.8 7.9 convolution_add_fusion
  439.2 9.4 fusion.63
  448.7 12.5 fusion.77
  461.3 14.5 %fusion.68 = f32[2048,3,512]{2,0,1:T(8,128)} fusion(bf16[1024,1,512]{2,0,1:T(8,128)(2,1)} %copy.45, bf16[1024,1,512]{2,0,1:T(8,128)(2,1)} %copy.44, bf16[1024,1,512]{2,0,1:T(8,128)(2,1)S(1)} %copy.43, bf16[1024,2048]{1,0:T(8,128)(2,1)} %param.15, f32[2048]{0:T(1024)S(1)} %copy-done.23, f32[2048]{0:T(1024)S(1)} %copy-done.19, f32[1024]{0:T(1024)S(1)} %copy-done.17, ...), kind=kOutput, calls=%fused_computation.128 | convolution fusion | flops 6464471040 | bytes 19947520 | tf_op jit(solution)/shard_map/td,tjc->djc/dot_general | solution.py:172
  475.8 2.0 convert_reduce_fusion.1
  477.8 213.4 %all-reduce.3.cloned.1.call-done = f32[1024,2048]{1,0:T(8,128)} async-done(((f32[1024,2048]{1,0:T(8,128)}), f32[1024,2048]{1,0:T(8,128)}) %all-reduce.3.cloned.1.call-update) | async-done | bytes 8388624 | tf_op jit(solution)/shard_map/psum | solution.py:183
  691.2 7.5 fusion.48
  698.7 26.3 %all-reduce = (f32[2048]{0:T(1024)}, f32[2048]{0:T(1024)}, f32[3,512]{1,0:T(4,128)}) all-reduce(f32[2048]{0:T(1024)S(1)} %get-tuple-element.231, f32[2048]{0:T(1024)S(1)} %get-tuple-element.234, f32[3,512]{1,0:T(4,128)S(1)} %convert_reduce_fusion.1), channel_id=1, replica_groups=mesh['dp'=8,'mp'=4] {'dp'}, use_global_device_ids=true, to_apply=%region_17.18 | all-reduce | flops 5632 | bytes 45056 | tf_op jit(solution)/shard_map/psum | solution.py:193
  725.1 6.7 copy.49
  731.8 521.4 %all-gather.3.cloned.1.call-done = f32[4096,2048]{1,0:T(8,128)} async-done(((f32[1024,2048]{1,0:T(8,128)}), f32[4096,2048]{1,0:T(8,128)}) %all-gather.3.cloned.1.call-update) | async-done | bytes 33554448 | tf_op jit(solution)/shard_map/all_gather | solution.py:128
  1253.2 15.9 %reduce_sum.112 = f32[1024,2048]{1,0:T(8,128)} reduce(f32[4,1024,2048]{2,1,0:T(8,128)} %bitcast.145, f32[]{:T(128)} %constant.41.clone.1), dimensions={0}, to_apply=%region_9.10 | reduce | flops 6291456 | bytes 41943044 | tf_op jit(solution)/shard_map/reduce_sum | solution.py:128
  1269.1 13.7 %fusion.47 = (bf16[1024,2048]{1,0:T(8,128)(2,1)}, bf16[1024,2048]{1,0:T(8,128)(2,1)}) fusion(bf16[1024,2048]{1,0:T(8,128)(2,1)} %param.15, bf16[1024,2048]{1,0:T(8,128)(2,1)} %param.25, f32[1024,2048]{1,0:T(8,128)} %all-reduce.3.cloned.1.call-done, f32[1024]{0:T(1024)S(1)} %broadcast_multiply_fusion, f32[1024]{0:T(1024)S(1)} %broadcast_multiply_fusion.1, ...), kind=kLoop, calls=%fused_computation.65 | loop fusion | flops 27262976 | bytes 33579008 | tf_op jit(solution)/shard_map/convert_element_type | solution.py:192
  (128 shorter events, 24.4 us)
Async XLA Ops:
  8.0 116.1 %copy-start = (bf16[512,2048]{1,0:T(8,128)(2,1)S(1)}, bf16[512,2048]{1,0:T(8,128)(2,1)}, u32[]{:S(2)}) copy-start(bf16[512,2048]{1,0:T(8,128)(2,1)} %param.22) | copy-start | bytes 6291460
  8.0 683.2 %all-reduce.3.cloned.1.call-start = ((), (), s32[]{:S(2)}) async-start(), calls=%async_computation.4 | async-start | bytes 16777216 | tf_op jit(solution)/shard_map/psum | solution.py:183
  8.1 3.6 copy-start.4
  11.7 10.1 copy-start.14
  12.9 8.9 copy-start.16
  13.0 8.9 copy-start.18
  13.0 8.9 copy-start.21
  13.0 8.9 copy-start.22
  32.4 4.1 copy-start.9
  40.8 1.4 copy-start.10
  40.8 1.4 copy-start.12
  45.3 78.8 %copy-start.20 = (bf16[1024]{0:T(1024)(128)(2,1)S(1)}, bf16[1024]{0:T(1024)(128)(2,1)}, u32[]{:S(2)}) copy-start(bf16[1024]{0:T(1024)(128)(2,1)} %fusion.65) | copy-start | bytes 6148
  54.3 4.3 copy-start.3
  93.6 4.3 copy-start.3
  136.0 9.7 copy-start.5
  159.4 11.4 copy-start.6
  179.6 2.7 copy-start.1
  184.2 1.3 copy-start.2
  211.3 9.7 copy-start.5
  234.8 11.4 copy-start.6
  255.5 2.7 copy-start.1
  260.1 1.3 copy-start.2
  283.5 6.5 copy-start.11
  283.5 6.5 copy-start.13
  316.2 15.2 %copy-start.15 = (f32[1024]{0:T(1024)S(1)}, f32[1024]{0:T(1024)}, u32[]{:S(2)}) copy-start(f32[1024]{0:T(1024)} %copy-done.14) | copy-start | bytes 12292
  316.2 15.2 %copy-start.17 = (f32[1024]{0:T(1024)S(1)}, f32[1024]{0:T(1024)}, u32[]{:S(2)}) copy-start(f32[1024]{0:T(1024)} %copy-done.16) | copy-start | bytes 12292
  316.2 15.2 %copy-start.19 = (f32[2048]{0:T(1024)S(1)}, f32[2048]{0:T(1024)}, u32[]{:S(2)}) copy-start(f32[2048]{0:T(1024)} %param.18) | copy-start | bytes 24580
  316.2 15.2 %copy-start.23 = (f32[2048]{0:T(1024)S(1)}, f32[2048]{0:T(1024)}, u32[]{:S(2)}) copy-start(f32[2048]{0:T(1024)} %param.19) | copy-start | bytes 24580
  331.4 35.8 %slice-start = ((s8[6291456]{0:T(1024)(128)(4,1)}), s8[4194304]{0:T(1024)(128)(4,1)S(1)}, s32[]{:S(2)}) async-start(s8[6291456]{0:T(1024)(128)(4,1)} %bitcast.152), calls=%async_computation.10 | async-start | bytes 8388608
  350.6 16.7 %slice-start.1 = ((s8[6291456]{0:T(1024)(128)(4,1)}), s8[2097152]{0:T(1024)(128)(4,1)S(1)}, s32[]{:S(2)}) async-start(s8[6291456]{0:T(1024)(128)(4,1)} %bitcast.152), calls=%async_computation.11 | async-start | bytes 4194304
  350.6 16.7 %copy-start.8 = (bf16[1024,1,512]{2,0,1:T(8,128)(2,1)S(1)}, bf16[1024,1,512]{2,0,1:T(8,128)(2,1)}, u32[]{:S(2)}) copy-start(bf16[1024,1,512]{2,0,1:T(8,128)(2,1)} %copy.44) | copy-start | bytes 3145732
  397.5 327.5 %reduce-scatter.9.cloned.1.call-start = ((), (), s32[]{:S(2)}) async-start(), calls=%async_computation.7 | async-start | bytes 25952256 | tf_op jit(solution)/shard_map/reduce_scatter | solution.py:177
  418.3 834.9 %all-gather.3.cloned.1.call-start = ((), (), s32[]{:S(2)}) async-start(), calls=%async_computation.9 | async-start | bytes 41943040 | tf_op jit(solution)/shard_map/all_gather | solution.py:128
  420.4 10.4 copy-start.7
  438.8 844.0 %reduce-scatter.7.cloned.1.call-start = ((), (), s32[]{:S(2)}) async-start(), calls=%async_computation.6 | async-start | bytes 4718592 | tf_op jit(solution)/shard_map/reduce_scatter | solution.py:176
  448.7 834.1 %reduce-scatter.11.cloned.1.call-start = ((), (), s32[]{:S(2)}) async-start(), calls=%async_computation.8 | async-start | bytes 12976128 | tf_op jit(solution)/shard_map/reduce_scatter | solution.py:178
  461.2 821.6 %reduce-scatter.5.cloned.1.call-start = ((), (), s32[]{:S(2)}) async-start(), calls=%async_computation.5 | async-start | bytes 14155776 | tf_op jit(solution)/shard_map/reduce_scatter | solution.py:175
Sparse Core Ops, SparseCore 0:
  397.7 293.5 all-reduce.2
  692.8 560.3 all-gather.2
Sparse Core Ops, SparseCore 1:
  418.4 148.9 reduce-scatter.8
  571.1 50.9 reduce-scatter.6
  626.0 86.9 reduce-scatter.10
  717.1 92.0 reduce-scatter.4
